TPU v7x, 256 devices: a whole 4x4x8 slice. The times are simulated.
256 devices in a mesh: wide: 32 (over x, z), blk: 8 (over y, core).
Axes of the slice: x: 4, y: 4, z: 8, core: 2. Of those that a mesh axis runs over, the one named last changes fastest.
Arguments:
- amplitudes: bfloat16 [32, 32, 32, 4096], P('blk', 'wide'), may hold values from -6 to 6
- integrals: bfloat16 [32, 2, 2048, 4096], P('wide', None, 'blk'), may hold values from -0.09375 to 0.09375
- owner: int32 [32], replicated, may hold values from 0 to 31, each once
- targets: int32 [32, 2], replicated, may hold values from 0 to 31, all different within a row
- counts: int32 [32], replicated, may hold values from 1 to 2, 48 in all
Outputs:
- ladder: bfloat16 [32, 32, 32, 2048], P(None, 'blk', 'wide')
Inputs may be any that keep to these rules, and one draw needn't show every extreme that they name: Each contracted tile has its own owner slot. `targets`: the output tiles of one contracted tile are distinct, and every output tile is named by some contracted tile. The counts sum to 48 and one of them is 2.
All inputs are finite; a program needn't handle non-finite values.
Results may differ from a plain program's by a relative error of at most 0.0044.
Values may be sent and summed in bfloat16 or wider, within the bound.
A program may use at most 128 MiB of HBM per device.

v0:
```python
import jax
import jax.numpy as jnp
from jax import lax
from jax.sharding import PartitionSpec as P


def body(amplitudes, integrals, owner, targets, counts):
    wide_count = lax.axis_size("wide")
    my_index = lax.axis_index("wide")
    tile_ids = jnp.arange(owner.shape[0], dtype=jnp.int32)
    holder = jnp.sum(jnp.where(owner[None, :] == tile_ids[:, None], tile_ids[None, :], 0), axis=1)
    ordered = jnp.take(amplitudes, holder, axis=2)
    my_tile = lax.all_to_all(ordered, "wide", split_axis=2, concat_axis=1, tiled=True)
    my_holder = lax.dynamic_index_in_dim(holder, my_index, 0, keepdims=False)
    my_count = lax.dynamic_index_in_dim(counts, my_holder, 0, keepdims=False)
    slot_ids = jnp.arange(targets.shape[1], dtype=jnp.int32)
    live_slots = (slot_ids < my_count).astype(jnp.float32)
    my_integrals = integrals[0]
    width = my_tile.shape[3]
    pair_rows = my_tile.reshape(-1, width)
    partial_value = jnp.einsum(
        "rc,kac->rka",
        pair_rows,
        lax.all_gather(my_integrals, "blk", axis=1, tiled=True),
        preferred_element_type=jnp.float32,
    )
    shaped = (partial_value * live_slots[None, :, None]).astype(jnp.bfloat16)
    shaped = shaped.reshape(my_tile.shape[0], my_tile.shape[1], targets.shape[1], shaped.shape[2])
    received = lax.all_to_all(shaped, "wide", split_axis=1, concat_axis=2, tiled=True)
    slot_targets = jnp.take(targets, holder, axis=0).reshape(-1)
    window_ids = jnp.arange(wide_count, dtype=jnp.int32)
    selector = (slot_targets[None, :] == window_ids[:, None]).astype(jnp.bfloat16)
    ladder = jnp.einsum("ps,ijsa->pija", selector, received, preferred_element_type=jnp.float32)
    return ladder.astype(jnp.bfloat16)


def solution(mesh):
    placed = (P("blk", "wide", None, None), P("wide", None, "blk", None), P(), P(), P())
    return jax.shard_map(
        body, mesh=mesh, in_specs=placed, out_specs=P(None, "blk", "wide", None), check_vma=False
    )
```

profile of v0, /device:TPU:8, one launch (start us, length us, event | category | flops | bytes accessed | tf_op | source)
XLA Modules:
  0.0 236.6 jit_solution(17188635275053602947)
XLA Ops:
  6.5 0.0 copy-start
  6.5 0.0 all-gather.3.cloned.1.call-start
  6.5 0.7 all-gather.3.cloned.1.call-update
  7.3 2.0 copy.32
  9.3 0.8 select_reduce_fusion
  10.1 1.4 gather_fusion.1
  11.6 1.5 fusion.9
  13.1 11.3 %all-to-all-start = ((bf16[4,1,32,4096]{3,0,1,2:T(4,128)(2,1)}), bf16[4,1,32,4096]{3,0,1,2:T(4,128)(2,1)S(1)}, u32[]{:S(2)}, u32[]{:S(2)}) async-start(bf16[4,1,32,4096]{3,0,1,2:T(4,128)(2,1)} %fusion.9), calls=%async_computation | async-start | bytes 2097152 | tf_op jit(solution)/shard_map/all_to_all | solution.py:13
  24.4 0.6 dynamic_slice.7
  27.0 1.3 dynamic_slice.8
  28.2 0.7 compare_convert_fusion
  28.9 24.1 %all-to-all-done = bf16[4,1,32,4096]{3,0,1,2:T(4,128)(2,1)S(1)} async-done(((bf16[4,1,32,4096]{3,0,1,2:T(4,128)(2,1)}), bf16[4,1,32,4096]{3,0,1,2:T(4,128)(2,1)S(1)}, u32[]{:S(2)}, u32[]{:S(2)}) %all-to-all-start) | async-done | bytes 1048608 | tf_op jit(solution)/shard_map/all_to_all | solution.py:13
  53.0 0.6 copy.24
  53.6 116.9 %all-gather.3.cloned.1.call-done = bf16[1,2,2048,4096]{3,2,1,0:T(8,128)(2,1)} async-done(((bf16[1,2,256,4096]{3,2,1,0:T(8,128)(2,1)}), bf16[1,2,2048,4096]{3,2,1,0:T(8,128)(2,1)}) %all-gather.3.cloned.1.call-update) | async-done | bytes 33554448 | tf_op jit(solution)/shard_map/all_gather | solution.py:24
  170.5 16.0 %fusion.5 = bf16[128,2,2048]{2,0,1:T(8,128)(2,1)S(1)} fusion(bf16[128,4096,1]{1,0,2:T(8,128)(2,1)S(1)} %bitcast.36, bf16[1,2,2048,4096]{3,2,1,0:T(8,128)(2,1)} %all-gather.3.cloned.1.call-done, f32[2]{0:T(128)S(1)} %compare_convert_fusion), kind=kOutput, calls=%fused_computation.6 | convolution fusion | flops 4296015872 | bytes 35651592 | tf_op jit(solution)/shard_map/rc,kac->rka/dot_general | solution.py:21
  186.6 1.8 copy.25
  188.3 9.8 %all-to-all-start.1 = ((bf16[4,32,2,2048]{3,0,2,1:T(4,128)(2,1)}), bf16[4,32,2,2048]{3,0,2,1:T(4,128)(2,1)S(1)}, u32[]{:S(2)}, u32[]{:S(2)}) async-start(bf16[4,32,2,2048]{3,0,2,1:T(4,128)(2,1)} %copy.25), calls=%async_computation.1 | async-start | bytes 2097152 | tf_op jit(solution)/shard_map/all_to_all | solution.py:29
  198.2 0.0 copy-done
  198.2 0.1 copy.21
  198.3 0.6 gather_fusion
  198.9 0.1 broadcast_select_fusion
  198.9 0.1 select_n.56
  199.0 28.2 %all-to-all-done.1 = bf16[4,32,2,2048]{3,0,2,1:T(4,128)(2,1)S(1)} async-done(((bf16[4,32,2,2048]{3,0,2,1:T(4,128)(2,1)}), bf16[4,32,2,2048]{3,0,2,1:T(4,128)(2,1)S(1)}, u32[]{:S(2)}, u32[]{:S(2)}) %all-to-all-start.1) | async-done | bytes 1048608 | tf_op jit(solution)/shard_map/all_to_all | solution.py:29
  227.2 1.3 fusion.8
  228.5 1.2 copy.27
  (3 shorter events, 0.0 us)
Async XLA Ops:
  6.5 191.7 %copy-start = (s32[32,2]{0,1:T(2,128)S(1)}, s32[32,2]{0,1:T(2,128)}, u32[]{:S(2)}) copy-start(s32[32,2]{0,1:T(2,128)} %param.8) | copy-start | bytes 772
  6.5 164.0 %all-gather.3.cloned.1.call-start = ((), (), s32[]{:S(2)}) async-start(), calls=%async_computation.2 | async-start | bytes 37748736 | tf_op jit(solution)/shard_map/all_gather | solution.py:24
  13.1 39.9 %all-to-all-start = ((bf16[4,1,32,4096]{3,0,1,2:T(4,128)(2,1)}), bf16[4,1,32,4096]{3,0,1,2:T(4,128)(2,1)S(1)}, u32[]{:S(2)}, u32[]{:S(2)}) async-start(bf16[4,1,32,4096]{3,0,1,2:T(4,128)(2,1)} %fusion.9), calls=%async_computation | async-start | bytes 2097152 | tf_op jit(solution)/shard_map/all_to_all | solution.py:13
  188.3 38.9 %all-to-all-start.1 = ((bf16[4,32,2,2048]{3,0,2,1:T(4,128)(2,1)}), bf16[4,32,2,2048]{3,0,2,1:T(4,128)(2,1)S(1)}, u32[]{:S(2)}, u32[]{:S(2)}) async-start(bf16[4,32,2,2048]{3,0,2,1:T(4,128)(2,1)} %copy.25), calls=%async_computation.1 | async-start | bytes 2097152 | tf_op jit(solution)/shard_map/all_to_all | solution.py:29
Sparse Core Ops, SparseCore 0:
  9.2 161.2 all-gather.2
where the time goes:
time: 237 us
  waiting for transfers between devices  170 us (72%)
  starting transfers between devices  21.2 us (9%)
  matrix products  17.3 us (7%)
  between operations  15.4 us (6%)
  local copies, waits for them, and re-layouts  9.66 us (4%)
  other arithmetic  3.06 us (1%)
    all_gather x1, waiting for transfers between devices, body(): lax.all_gather(my_integrals, 'blk', axis=1, tiled=True)  117 us
    all_to_all x1, waiting for transfers between devices, body(): lax.all_to_all(shaped, 'wide', split_axis=1, concat_axis=2, tiled=True)  28.2 us
    all_to_all x1, waiting for transfers between devices, body(): lax.all_to_all(ordered, 'wide', split_axis=2, concat_axis=1, tiled=True)  24.1 us
    dot_general x1, matrix products, body(): jnp.einsum('rc,kac->rka', pair_rows, lax.all_gather(my_integrals, 'blk',...  16 us
    all_to_all x1, starting transfers between devices, body(): lax.all_to_all(ordered, 'wide', split_axis=2, concat_axis=1, tiled=True)  11.3 us
    all_to_all x1, starting transfers between devices, body(): lax.all_to_all(shaped, 'wide', split_axis=1, concat_axis=2, tiled=True)  9.84 us
  transfers between devices with their start and end apart: 3, of which 3 were waited for; matrix products, arithmetic and copies ran while one was open for 4% of the time, Pallas kernels for 0%

commit v1 on v0

--- a/solution.py
+++ b/solution.py
@@ -21,7 +21,9 @@
     partial_value = jnp.einsum(
         "rc,kac->rka",
         pair_rows,
-        lax.all_gather(my_integrals, "blk", axis=1, tiled=True),
+        jnp.concatenate(
+            lax.all_to_all(jnp.stack([my_integrals] * lax.axis_size("blk")), "blk", 0, 0), axis=1
+        ),
         preferred_element_type=jnp.float32,
     )
     shaped = (partial_value * live_slots[None, :, None]).astype(jnp.bfloat16)

time: 237 us -> 505 us (2.13)
  waiting for transfers between devices: 170 us -> 386 us
  blocking collectives: 0 us -> 39.7 us
  local copies, waits for them, and re-layouts: 9.66 us -> 44.3 us
  between operations: 15.4 us -> 2.04 us
  starting transfers between devices: 21.2 us -> 12.6 us
    all_to_all x1, waiting for transfers between devices: 24.1 us -> 359 us  [body(): lax.all_to_all(jnp.stack([my_integrals] * lax.axis_size('blk')), 'blk', 0...]
    all_gather x1 -> x0, waiting for transfers between devices: 117 us -> none  [body(): lax.all_gather(my_integrals, 'blk', axis=1, tiled=True)]
    all_to_all x0 -> x1, blocking collectives: none -> 39.7 us  [body(): lax.all_to_all(ordered, 'wide', split_axis=2, concat_axis=1, tiled=True)]
    reshape x0 -> x1, local copies, waits for them, and re-layouts: none -> 22.9 us  [body(): jnp.concatenate(lax.all_to_all(jnp.stack([my_integrals] * lax.axis_size('...]
    another operation x0 -> x1, local copies, waits for them, and re-layouts: none -> 12.4 us  [body(): jnp.stack([my_integrals] * lax.axis_size('blk'))]
  transfers between devices with their start and end apart: 3 -> 2, of which waited for: 3 -> 2; matrix products, arithmetic and copies ran while one was open for 4% -> 1% of each run, Pallas kernels for 0% -> 0%
where the time goes in v1:
time: 505 us; the launch traced here: 504 us
  waiting for transfers between devices  386 us (76%)
  local copies, waits for them, and re-layouts  44.3 us (9%)
  blocking collectives  39.7 us (8%)
  matrix products  17.4 us (3%)
  starting transfers between devices  12.6 us (2%)
    all_to_all x1, waiting for transfers between devices, body(): lax.all_to_all(jnp.stack([my_integrals] * lax.axis_size('blk')), 'blk', 0...  359 us
    all_to_all x1, blocking collectives, body(): lax.all_to_all(ordered, 'wide', split_axis=2, concat_axis=1, tiled=True)  39.7 us
    all_to_all x1, waiting for transfers between devices, body(): lax.all_to_all(shaped, 'wide', split_axis=1, concat_axis=2, tiled=True)  27.6 us
    reshape x1, local copies, waits for them, and re-layouts, body(): jnp.concatenate(lax.all_to_all(jnp.stack([my_integrals] * lax.axis_size('...  22.9 us
    dot_general x1, matrix products, body(): jnp.einsum('rc,kac->rka', pair_rows, jnp.concatenate(lax.all_to_all(jnp.s...  16.1 us
    another operation x1, local copies, waits for them, and re-layouts, body(): jnp.stack([my_integrals] * lax.axis_size('blk'))  12.4 us
  transfers between devices with their start and end apart: 2, of which 2 were waited for; matrix products, arithmetic and copies ran while one was open for 1% of the time, Pallas kernels for 0%

profile of v1, /device:TPU:8, one launch (start us, length us, event | category | flops | bytes accessed | tf_op | source)
XLA Modules:
  0.0 504.3 jit_solution(6126716716485154112)
XLA Ops:
  0.0 0.8 select_reduce_fusion
  0.8 2.0 copy.34
  2.8 1.4 gather_fusion.1
  4.3 0.6 fusion.2
  4.9 39.7 %all_to_all.23 = bf16[4,1,32,4096]{3,0,1,2:T(4,128)(2,1)S(1)} all-to-all(bf16[4,1,32,4096]{3,0,1,2:T(4,128)(2,1)S(1)} %fusion.2), channel_id=1, replica_groups=mesh['wide'=32,'blk'=8] {'wide'}, dimensions={2} | all-to-all | bytes 2097152 | tf_op jit(solution)/shard_map/all_to_all | solution.py:13
  44.6 12.4 %stack.3 = bf16[8,2,256,4096]{3,2,1,0:T(8,128)(2,1)} broadcast(bf16[2,256,4096]{2,1,0:T(8,128)(2,1)} %bitcast.35), dimensions={1,2,3} | broadcast | bytes 37748736 | tf_op jit(solution)/shard_map/stack | solution.py:25
  57.0 0.0 copy-start.1
  57.0 7.5 %all-to-all-start.1 = ((bf16[8,2,256,4096]{3,2,1,0:T(8,128)(2,1)}), bf16[8,2,256,4096]{3,2,1,0:T(8,128)(2,1)}, u32[]{:S(2)}, u32[]{:S(2)}) async-start(bf16[8,2,256,4096]{3,2,1,0:T(8,128)(2,1)} %stack.3), calls=%async_computation.1 | async-start | bytes 67108864 | tf_op jit(solution)/shard_map/all_to_all | solution.py:25
  64.5 0.6 dynamic_slice.7
  67.1 0.0 copy-done.1
  67.1 0.6 dynamic_slice.8
  67.7 0.6 compare_convert_fusion
  68.3 0.6 copy.25
  68.9 358.5 %all-to-all-done.1 = bf16[8,2,256,4096]{3,2,1,0:T(8,128)(2,1)} async-done(((bf16[8,2,256,4096]{3,2,1,0:T(8,128)(2,1)}), bf16[8,2,256,4096]{3,2,1,0:T(8,128)(2,1)}, u32[]{:S(2)}, u32[]{:S(2)}) %all-to-all-start.1) | async-done | bytes 33554464 | tf_op jit(solution)/shard_map/all_to_all | solution.py:25
  427.5 22.9 %copy.26 = bf16[2,8,256,4096]{3,2,1,0:T(8,128)(2,1)} copy(bf16[2,8,256,4096]{3,2,0,1:T(8,128)(2,1)} %bitcast.10) | data formatting | bytes 67108864 | tf_op jit(solution)/shard_map/reshape | solution.py:24
  450.4 0.0 copy-start
  450.4 16.1 %fusion = bf16[128,2,2048]{2,0,1:T(8,128)(2,1)S(1)} fusion(bf16[128,4096,1]{1,0,2:T(8,128)(2,1)S(1)} %bitcast.34, bf16[2,2048,4096]{2,1,0:T(8,128)(2,1)} %bitcast.32, f32[2]{0:T(128)S(1)} %compare_convert_fusion), kind=kOutput, calls=%fused_computation.3 | convolution fusion | flops 4296015872 | bytes 35651592 | tf_op jit(solution)/shard_map/rc,kac->rka/dot_general | solution.py:21
  466.4 1.8 copy.27
  468.2 5.1 %all-to-all-start.2 = ((bf16[4,32,2,2048]{3,0,2,1:T(4,128)(2,1)}), bf16[4,32,2,2048]{3,0,2,1:T(4,128)(2,1)S(1)}, u32[]{:S(2)}, u32[]{:S(2)}) async-start(bf16[4,32,2,2048]{3,0,2,1:T(4,128)(2,1)} %copy.27), calls=%async_computation.2 | async-start | bytes 2097152 | tf_op jit(solution)/shard_map/all_to_all | solution.py:31
  473.3 0.0 copy-done
  473.3 0.1 copy.22
  473.4 0.6 gather_fusion
  474.0 0.1 broadcast_select_fusion
  474.1 0.1 select_n.56
  474.2 27.6 %all-to-all-done.2 = bf16[4,32,2,2048]{3,0,2,1:T(4,128)(2,1)S(1)} async-done(((bf16[4,32,2,2048]{3,0,2,1:T(4,128)(2,1)}), bf16[4,32,2,2048]{3,0,2,1:T(4,128)(2,1)S(1)}, u32[]{:S(2)}, u32[]{:S(2)}) %all-to-all-start.2) | async-done | bytes 1048608 | tf_op jit(solution)/shard_map/all_to_all | solution.py:31
  501.8 1.3 fusion.1
  503.1 1.2 copy.29
  (3 shorter events, 0.0 us)
Async XLA Ops:
  57.0 10.1 %copy-start.1 = (s32[32]{0:T(128)S(1)}, s32[32]{0:T(128)}, u32[]{:S(2)}) copy-start(s32[32]{0:T(128)} %param.9) | copy-start | bytes 388
  57.0 370.5 %all-to-all-start.1 = ((bf16[8,2,256,4096]{3,2,1,0:T(8,128)(2,1)}), bf16[8,2,256,4096]{3,2,1,0:T(8,128)(2,1)}, u32[]{:S(2)}, u32[]{:S(2)}) async-start(bf16[8,2,256,4096]{3,2,1,0:T(8,128)(2,1)} %stack.3), calls=%async_computation.1 | async-start | bytes 67108864 | tf_op jit(solution)/shard_map/all_to_all | solution.py:25
  450.4 23.0 %copy-start = (s32[32,2]{0,1:T(2,128)S(1)}, s32[32,2]{0,1:T(2,128)}, u32[]{:S(2)}) copy-start(s32[32,2]{0,1:T(2,128)} %param.8) | copy-start | bytes 772
  468.2 33.6 %all-to-all-start.2 = ((bf16[4,32,2,2048]{3,0,2,1:T(4,128)(2,1)}), bf16[4,32,2,2048]{3,0,2,1:T(4,128)(2,1)S(1)}, u32[]{:S(2)}, u32[]{:S(2)}) async-start(bf16[4,32,2,2048]{3,0,2,1:T(4,128)(2,1)} %copy.27), calls=%async_computation.2 | async-start | bytes 2097152 | tf_op jit(solution)/shard_map/all_to_all | solution.py:31
